TPU v7x, 512 devices: a whole 4x8x8 slice. The times are simulated.
512 devices in a mesh: scalp: 256 (over z, y, x), screen: 2 (over core).
Axes of the slice: x: 4, y: 8, z: 8, core: 2. Of those that a mesh axis runs over, the one named last changes fastest.
Arguments:
- guides: bfloat16 [1048576, 384], P('scalp'), may hold values from -6 to 6
- neighbours: int32 [2048, 32], P(('scalp', 'screen')), may hold values from 0 to 1048575, as said below
- pick: int32 [2048, 4, 256], P(('scalp', 'screen')), may hold values from 0 to 31, as said below
- pick_weight: bfloat16 [2048, 4, 256], P(('scalp', 'screen')), may hold values from 0.099609375 to 0.59765625
- keep: int32 [2048, 256], P(('scalp', 'screen')), may hold values 0 or 1
- width: float32 [2048, 256], P(('scalp', 'screen')), may hold values from 0.2 to 2
- route: int32 [2048, 1], P(('scalp', 'screen')), may hold values from 0 to 1; in each aligned block of 4 rows (0 to 3, 4 to 7, ...) at most 3 rows name the same one
- tess_centre: bfloat16 [2, 384, 768], P('screen'), may hold values from -0.3125 to 0.3125
- tess_side: bfloat16 [2, 384, 768], P('screen'), may hold values from -0.3125 to 0.3125
Outputs:
- ribbon: bfloat16 [786432, 768], P(('scalp', 'screen'))
Inputs may be any that keep to these rules, and one draw needn't show every extreme that they name: `neighbours`: each entry names a guide of the render block's own scalp tile or of the scalp tile just before or after it, wrapping around; a block of device (s, c) belongs to scalp tile s. `pick`: the 4 entries of one render strand differ. `route`: among the 4 blocks of one device at most 3 name the same screen tile.
All inputs are finite; a program needn't handle non-finite values. No bound on the sum of `keep` on one device may be relied on, other than what follows from the above.
Results may differ from a plain program's by a relative error of at most 0.009.
Values may be sent and summed in bfloat16 or wider, within the bound.
No kernel may reach another device: no remote copies, remote signals or barrier semaphores. Data moves between devices by JAX's collectives and lax.ppermute only.
A program may use at most 64 MiB of HBM per device.

v0:
```python
import jax
import jax.numpy as jnp
from jax import lax
from jax.sharding import PartitionSpec as P


def extended(block, sides, width):
    for axis, dim in sides:
        count = lax.axis_size(axis)
        forward = [(i, i + 1) for i in range(count - 1)]
        forward.append((count - 1, 0))
        backward = [(target, source) for source, target in forward]
        low = lax.ppermute(
            lax.slice_in_dim(block, block.shape[dim] - width, None, axis=dim), axis, forward
        )
        high = lax.ppermute(lax.slice_in_dim(block, 0, width, axis=dim), axis, backward)
        block = jnp.concatenate([low, block, high], axis=dim)
    return block


def blend(picks, weights, count):
    hit = (picks[..., None] == jnp.arange(count, dtype=jnp.int32)).astype(jnp.float32)
    return jnp.sum(hit * weights.astype(jnp.float32)[..., None], axis=1).astype(jnp.bfloat16)


def shards(guides, neighbours, pick, pick_weight, keep, width, route, tess_centre, tess_side):
    scalps = lax.axis_size("scalp")
    screens = lax.axis_size("screen")
    tile = guides.shape[0]
    blocks = neighbours.shape[0]
    listed = neighbours.shape[1]
    strands = keep.shape[1]
    slots_each = blocks // screens + blocks // 4
    centre_map = tess_centre[0]
    side_map = tess_side[0]
    here = lax.axis_index("scalp")
    owner = neighbours // tile
    relative = jnp.mod(owner - here + 1, scalps)
    window = extended(guides, (("scalp", 0),), tile)
    gathered = window[relative * tile + neighbours % tile]
    mixing = blend(pick, pick_weight, listed)
    kept = keep.astype(jnp.float32)
    scaled = width * strands / (jnp.sum(kept, axis=1, keepdims=True) + 1.0)
    tiles = route[:, 0]
    same = tiles[:, None] == tiles[None, :]
    earlier = jnp.arange(blocks)[None, :] < jnp.arange(blocks)[:, None]
    rank = jnp.sum(same & earlier, axis=1)
    slot = tiles * slots_each + rank
    select = slot[None, :] == jnp.arange(screens * slots_each, dtype=jnp.int32)[:, None]
    select_half = select.astype(jnp.bfloat16)
    select_full = select.astype(jnp.float32)
    kept_packed = jnp.dot(select_full, kept, precision=lax.Precision.HIGHEST).reshape(
        screens, slots_each, strands
    )
    scaled_packed = jnp.dot(select_full, scaled, precision=lax.Precision.HIGHEST).reshape(
        screens, slots_each, strands
    )
    panel = jnp.einsum("rbk,rkx->rbx", mixing, gathered, preferred_element_type=jnp.float32).astype(
        jnp.bfloat16
    )
    panel_packed = jnp.einsum(
        "sr,rbx->sbx", select_half, panel, preferred_element_type=jnp.float32
    ).astype(jnp.bfloat16)
    panel_packed = panel_packed.reshape(screens, slots_each, strands, panel.shape[2])
    panel = lax.all_to_all(panel_packed, "screen", split_axis=0, concat_axis=0, tiled=True)
    flat = panel.reshape(-1, panel.shape[-1])
    centre = jnp.dot(flat, centre_map, preferred_element_type=jnp.float32)
    side = jnp.dot(flat, side_map, preferred_element_type=jnp.float32)
    vertex = lax.all_to_all(
        kept_packed.astype(jnp.bfloat16), "screen", split_axis=0, concat_axis=0, tiled=True
    ).astype(kept_packed.dtype).reshape(-1, 1) * (
        centre
        + lax.all_to_all(
            scaled_packed.astype(jnp.bfloat16), "screen", split_axis=0, concat_axis=0, tiled=True
        )
        .astype(scaled_packed.dtype)
        .reshape(-1, 1)
        * side
    )
    received = vertex.astype(jnp.bfloat16).reshape(panel.shape[:3] + (centre.shape[1],))
    return received.reshape(-1, received.shape[-1])


def solution(mesh):
    return jax.shard_map(
        shards,
        mesh=mesh,
        in_specs=(
            P("scalp", None),
            P(("scalp", "screen"), None),
            P(("scalp", "screen"), None, None),
            P(("scalp", "screen"), None, None),
            P(("scalp", "screen"), None),
            P(("scalp", "screen"), None),
            P(("scalp", "screen"), None),
            P("screen", None, None),
            P("screen", None, None),
        ),
        out_specs=P(("scalp", "screen"), None),
        check_vma=False,
    )
```

profile of v0, /device:TPU:1, one launch (start us, length us, event | category | flops | bytes accessed | tf_op | source)
XLA Modules:
  0.0 125.2 jit_solution(10222333162345851337)
XLA Ops:
  0.0 0.0 copy-start
  0.0 16.7 %collective-permute-start.1 = (bf16[4096,384]{1,0:T(8,128)(2,1)}, bf16[4096,384]{1,0:T(8,128)(2,1)}, u32[]{:S(2)}, u32[]{:S(2)}) collective-permute-start(bf16[4096,384]{1,0:T(8,128)(2,1)} %param.9), channel_id=1, source_target_pairs={{2,0},{4,2},{6,4},{8,6},{10,8},{12,10},{14,12},{16,14},{18,16},{20... | collective-permute-start | bytes 9437192 | tf_op jit(solution)/shard_map/ppermute | solution.py:16
  16.7 1.9 %collective-permute-start = (bf16[4096,384]{1,0:T(8,128)(2,1)}, bf16[4096,384]{1,0:T(8,128)(2,1)}, u32[]{:S(2)}, u32[]{:S(2)}) collective-permute-start(bf16[4096,384]{1,0:T(8,128)(2,1)} %param.9), channel_id=1, source_target_pairs={{0,2},{2,4},{4,6},{6,8},{8,10},{10,12},{12,14},{14,16},{16,18},{18... | collective-permute-start | bytes 9437192 | tf_op jit(solution)/shard_map/ppermute | solution.py:13
  18.7 0.8 convert_reduce_fusion
  19.5 0.9 convert_reduce_fusion.1
  20.4 0.7 multiply_add_fusion
  21.0 0.9 convolution_convert_fusion.2
  22.0 0.6 convert_element_type.47
  22.6 4.2 %all-to-all-start.2 = ((bf16[2,3,256]{2,1,0:T(4,128)(2,1)}), bf16[2,3,256]{2,1,0:T(4,128)(2,1)S(1)}, u32[]{:S(2)}, u32[]{:S(2)}) async-start(bf16[2,3,256]{2,1,0:T(4,128)(2,1)} %convert_element_type.47), calls=%async_computation.2 | async-start | bytes 8192 | tf_op jit(solution)/shard_map/all_to_all | solution.py:73
  26.8 0.7 compare_select_fusion
  27.5 0.1 reshape.35
  27.5 0.7 convert_element_type.42
  28.2 0.9 convolution_convert_fusion.3
  29.2 0.6 convert_element_type.41
  29.8 0.0 all-to-all-done.2
  29.8 3.2 %all-to-all-start = ((bf16[2,3,256]{2,1,0:T(4,128)(2,1)}), bf16[2,3,256]{2,1,0:T(4,128)(2,1)S(1)}, u32[]{:S(2)}, u32[]{:S(2)}) async-start(bf16[2,3,256]{2,1,0:T(4,128)(2,1)} %convert_element_type.41), calls=%async_computation | async-start | bytes 8192 | tf_op jit(solution)/shard_map/all_to_all | solution.py:69
  33.1 1.0 all-to-all-done
  34.1 0.8 select_reduce_fusion
  34.9 48.9 %collective-permute-done.1 = bf16[4096,384]{1,0:T(8,128)(2,1)} collective-permute-done((bf16[4096,384]{1,0:T(8,128)(2,1)}, bf16[4096,384]{1,0:T(8,128)(2,1)}, u32[]{:S(2)}, u32[]{:S(2)}) %collective-permute-start.1) | collective-permute-done | bytes 3145760 | tf_op jit(solution)/shard_map/ppermute | solution.py:16
  83.8 9.3 %collective-permute-done = bf16[4096,384]{1,0:T(8,128)(2,1)} collective-permute-done((bf16[4096,384]{1,0:T(8,128)(2,1)}, bf16[4096,384]{1,0:T(8,128)(2,1)}, u32[]{:S(2)}, u32[]{:S(2)}) %collective-permute-start) | collective-permute-done | bytes 3145760 | tf_op jit(solution)/shard_map/ppermute | solution.py:13
  93.1 14.6 %pad_maximum_fusion = bf16[12288,384]{1,0:T(8,128)(2,1)} fusion(bf16[4096,384]{1,0:T(8,128)(2,1)} %collective-permute-done.1, bf16[4096,384]{1,0:T(8,128)(2,1)} %param.9, bf16[4096,384]{1,0:T(8,128)(2,1)} %collective-permute-done), kind=kLoop, calls=%fused_computation.1 | loop fusion | flops 28311552 | bytes 18874368 | tf_op jit(solution)/shard_map/concatenate | solution.py:17
  107.7 5.7 %gather_fusion = bf16[128,384]{1,0:T(8,128)(2,1)S(1)} fusion(bf16[12288,384]{1,0:T(8,128)(2,1)} %pad_maximum_fusion, s32[1024]{0:T(1024)S(1)} %pad_clamp_fusion), kind=kCustom, calls=%fused_computation | custom fusion | bytes 197120 | tf_op jit(solution)/shard_map/gather | solution.py:40
  113.4 0.4 convolution_convert_fusion.1
  113.8 0.9 convolution_convert_fusion
  114.7 0.2 copy.12
  114.8 6.1 %all_to_all.15 = bf16[2,3,256,384]{3,2,1,0:T(8,128)(2,1)S(1)} all-to-all(bf16[2,3,256,384]{3,2,1,0:T(8,128)(2,1)S(1)} %bitcast.20), channel_id=1, replica_groups=mesh['scalp'=256,'screen'=2] {'screen'}, dimensions={0} | all-to-all | bytes 2359296 | tf_op jit(solution)/shard_map/all_to_all | solution.py:65
  121.0 0.0 copy-done
  121.0 0.0 copy-start.1
  121.0 1.4 %fusion.2 = f32[1536,768]{1,0:T(8,128)S(1)} fusion(bf16[1536,384]{1,0:T(8,128)(2,1)S(1)} %bitcast.18, bf16[1,384,768]{2,1,0:T(8,128)(2,1)S(1)} %copy-done), kind=kOutput, calls=%fused_computation.9 | convolution fusion | flops 905969664 | bytes 6488064 | tf_op jit(solution)/shard_map/dot_general | solution.py:67
  122.4 0.0 copy-done.1
  122.4 2.8 %multiply_convert_fusion = bf16[1536,768]{1,0:T(8,128)(2,1)} fusion(f32[1536,768]{1,0:T(8,128)S(1)} %fusion.2, bf16[1536,384]{1,0:T(8,128)(2,1)S(1)} %bitcast.19, f32[1536]{0:T(1024)S(1)} %reshape.32, f32[1536]{0:T(1024)S(1)} %reshape.31, bf16[1,384,768]{2,1,0:T(8,128)(2,1)S(1)} %copy-done.1), kind=kOutput, calls=%fused_computation.2 | convolution fusion | flops 910688256 | bytes 8859648 | tf_op jit(solution)/shard_map/dot_general | solution.py:68
  (4 shorter events, 0.0 us)
Async XLA Ops:
  0.0 121.0 %copy-start = (bf16[1,384,768]{2,1,0:T(8,128)(2,1)S(1)}, bf16[1,384,768]{2,1,0:T(8,128)(2,1)}, u32[]{:S(2)}) copy-start(bf16[1,384,768]{2,1,0:T(8,128)(2,1)} %param.16) | copy-start | bytes 1769476
  0.0 83.8 %collective-permute-start.1 = (bf16[4096,384]{1,0:T(8,128)(2,1)}, bf16[4096,384]{1,0:T(8,128)(2,1)}, u32[]{:S(2)}, u32[]{:S(2)}) collective-permute-start(bf16[4096,384]{1,0:T(8,128)(2,1)} %param.9), channel_id=1, source_target_pairs={{2,0},{4,2},{6,4},{8,6},{10,8},{12,10},{14,12},{16,14},{18,16},{20... | collective-permute-start | bytes 9437192 | tf_op jit(solution)/shard_map/ppermute | solution.py:16
  16.7 76.3 %collective-permute-start = (bf16[4096,384]{1,0:T(8,128)(2,1)}, bf16[4096,384]{1,0:T(8,128)(2,1)}, u32[]{:S(2)}, u32[]{:S(2)}) collective-permute-start(bf16[4096,384]{1,0:T(8,128)(2,1)} %param.9), channel_id=1, source_target_pairs={{0,2},{2,4},{4,6},{6,8},{8,10},{10,12},{12,14},{14,16},{16,18},{18... | collective-permute-start | bytes 9437192 | tf_op jit(solution)/shard_map/ppermute | solution.py:13
  22.6 7.2 %all-to-all-start.2 = ((bf16[2,3,256]{2,1,0:T(4,128)(2,1)}), bf16[2,3,256]{2,1,0:T(4,128)(2,1)S(1)}, u32[]{:S(2)}, u32[]{:S(2)}) async-start(bf16[2,3,256]{2,1,0:T(4,128)(2,1)} %convert_element_type.47), calls=%async_computation.2 | async-start | bytes 8192 | tf_op jit(solution)/shard_map/all_to_all | solution.py:73
  29.8 4.3 %all-to-all-start = ((bf16[2,3,256]{2,1,0:T(4,128)(2,1)}), bf16[2,3,256]{2,1,0:T(4,128)(2,1)S(1)}, u32[]{:S(2)}, u32[]{:S(2)}) async-start(bf16[2,3,256]{2,1,0:T(4,128)(2,1)} %convert_element_type.41), calls=%async_computation | async-start | bytes 8192 | tf_op jit(solution)/shard_map/all_to_all | solution.py:69
  121.0 1.4 %copy-start.1 = (bf16[1,384,768]{2,1,0:T(8,128)(2,1)S(1)}, bf16[1,384,768]{2,1,0:T(8,128)(2,1)}, u32[]{:S(2)}) copy-start(bf16[1,384,768]{2,1,0:T(8,128)(2,1)} %param.17) | copy-start | bytes 1769476
where the time goes:
time: 126 us; the launch traced here: 125 us
  waiting for transfers between devices  59.2 us (47%)
  starting transfers between devices  26 us (21%)
  other arithmetic  19.2 us (15%)
  matrix products  7.36 us (6%)
  local copies, waits for them, and re-layouts  7.24 us (6%)
  blocking collectives  6.12 us (5%)
    ppermute x1, waiting for transfers between devices, extended(): lax.ppermute(lax.slice_in_dim(block, 0, width, axis=dim), axis, backward)  48.9 us
    ppermute x1, starting transfers between devices, extended(): lax.ppermute(lax.slice_in_dim(block, 0, width, axis=dim), axis, backward)  16.7 us
    concatenate x1, other arithmetic, extended(): block = jnp.concatenate([low, block, high], axis=dim)  14.6 us
    ppermute x1, waiting for transfers between devices, extended(): lax.ppermute(lax.slice_in_dim(block, block.shape[dim] - width, None, axis...  9.27 us
    all_to_all x1, blocking collectives, shards(): lax.all_to_all(panel_packed, 'screen', split_axis=0, concat_axis=0, tiled...  6.12 us
    gather x1, local copies, waits for them, and re-layouts, shards(): gathered = window[relative * tile + neighbours % tile]  5.74 us
    all_to_all x1, starting transfers between devices, shards(): lax.all_to_all(scaled_packed.astype(jnp.bfloat16), 'screen', split_axis=0...  4.17 us
    all_to_all x1, starting transfers between devices, shards(): lax.all_to_all(kept_packed.astype(jnp.bfloat16), 'screen', split_axis=0,...  3.23 us
  transfers between devices with their start and end apart: 4, of which 3 were waited for; matrix products, arithmetic and copies ran while one was open for 6% of the time, Pallas kernels for 0%

commit v1 on v0

v1 whole, which is shorter than its diff:
```python
import functools

import jax
import jax.numpy as jnp
from jax import lax
from jax.experimental import pallas as pl
from jax.experimental.pallas import tpu as pltpu
from jax.sharding import PartitionSpec as P

F32 = jnp.float32
BF16 = jnp.bfloat16
VMEM = pl.BlockSpec(memory_space=pltpu.VMEM)
SMEM = pl.BlockSpec(memory_space=pltpu.SMEM)
CHUNK = 256
LIMIT = 16 * 1024 * 1024


def iota(shape, dim):
    return lax.broadcasted_iota(jnp.int32, shape, dim)


def fill_hot(hot_ref, index, valid):
    rows = index.shape[0]
    high = jnp.floor(index * (1.0 / CHUNK))
    low = index - high * CHUNK
    low = low if valid is None else jnp.where(valid, low, -1.0)
    lanes = iota((rows, CHUNK), 1).astype(F32)
    for part in range(hot_ref.shape[1] // CHUNK):
        key = jnp.where(high == part, low, -1.0)
        hot_ref[:, part * CHUNK : (part + 1) * CHUNK] = jnp.where(key == lanes, 1.0, 0.0).astype(BF16)


def serve_kernel(ask_ref, table_ref, out_ref, hot_ref):
    blocks, listed = ask_ref.shape
    tile = table_ref.shape[0]
    within = jnp.bitwise_and(ask_ref[...], tile - 1).astype(F32)
    wide = jnp.concatenate(
        [jnp.broadcast_to(within[b : b + 1, :], (listed, listed)) for b in range(blocks)], axis=0
    )
    on = jnp.bitwise_and(iota(wide.shape, 0), listed - 1) == iota(wide.shape, 1)
    index = jnp.sum(jnp.where(on, wide, 0.0), axis=1, keepdims=True)
    fill_hot(hot_ref, index, None)
    out_ref[...] = jnp.dot(hot_ref[...], table_ref[...], preferred_element_type=F32).astype(BF16)


def pack_kernel(route_ref, pick_ref, weight_ref, keep_ref, width_ref, after_ref, out_ref):
    blocks, picks, strands = pick_ref.shape
    del after_ref
    for b in range(blocks):
        tile = route_ref[b]
        rank = jnp.int32(0)
        for e in range(b):
            rank = rank + jnp.where(route_ref[e] == tile, 1, 0)
        kept = keep_ref[b : b + 1, :].astype(F32)
        scaled = width_ref[b : b + 1, :] * strands / (jnp.sum(kept, axis=1, keepdims=True) + 1.0)
        out_ref[b, 0:picks, :] = pick_ref[b].astype(F32)
        out_ref[b, picks : 2 * picks, :] = weight_ref[b].astype(F32)
        out_ref[b, 8:9, :] = kept
        out_ref[b, 9:10, :] = kept * scaled
        out_ref[b, 10:11, :] = jnp.full((1, strands), tile.astype(F32))
        out_ref[b, 11:12, :] = jnp.full((1, strands), rank.astype(F32))
        out_ref[b, 12:16, :] = jnp.zeros((4, strands), F32)


def plan_kernel(ask_ref, mine_ref, theirs_ref, table_ref, own_ref, sel_r_ref, sel_x_ref, mix_ref, hot_ref, *, scalps, slots):
    blocks, listed = ask_ref.shape
    half = blocks // 2
    tile = table_ref.shape[0]
    core = lax.axis_index("screen")
    here = lax.axis_index("scalp")
    strands = mine_ref.shape[2]
    lanes = blocks * listed
    core_f = core.astype(F32)
    codes = []
    for group, ref in enumerate((mine_ref, theirs_ref)):
        for b in range(half):
            goes = ref[b, 10:11, :] == core_f
            codes.append(jnp.where(goes, ref[b, 11:12, :], -1.0))
        for q in range(slots):
            packed = jnp.zeros((16, strands), F32)
            for b in range(half):
                packed = packed + jnp.where(codes[group * half + b] == q, ref[b], 0.0)
            spread = jnp.zeros((listed, strands), F32)
            row = iota((listed, strands), 0).astype(F32)
            for j in range(4):
                spread = spread + jnp.where(row == packed[j : j + 1, :], packed[4 + j : 5 + j, :], 0.0)
            both = jnp.concatenate([spread * packed[8:9, :], spread * packed[9:10, :]], axis=0)
            mix_ref[group * slots + q] = both.T.astype(BF16)
    ask = jnp.concatenate([ask_ref[...]] * blocks, axis=1)
    at = iota((blocks, lanes), 0) == iota((blocks, lanes), 1) // listed
    owner = ask // tile
    relative = owner - here + 1
    relative = jnp.where(relative < 0, relative + scalps, relative)
    relative = jnp.where(relative >= scalps, relative - scalps, relative)
    relative = jnp.sum(jnp.where(at, relative, 0).astype(F32), axis=0, keepdims=True)
    within = jnp.sum(jnp.where(at, jnp.bitwise_and(ask, tile - 1), 0).astype(F32), axis=0, keepdims=True)
    block_of = iota((1, lanes), 1) // listed
    code = jnp.zeros((1, lanes), F32)
    for b in range(blocks):
        code = code + jnp.where(block_of == b, codes[b][:, :lanes], 0.0)
    rows = 2 * slots * listed
    r = iota((rows, lanes), 0)
    l = iota((rows, lanes), 1)
    base = (r % listed == l % listed) & (r // (slots * listed) == l // (half * listed))
    base = base & (((r // listed) % slots).astype(F32) == code)
    near = 2.0 - 2.0 * core_f
    sel_r = jnp.where(base & (relative == near), 1.0, 0.0)
    sel_x = jnp.where(base & (relative == 2.0 - near), 1.0, 0.0)
    sel_o = jnp.where(base & (relative == 1.0), 1.0, 0.0)
    sel_r_ref[...] = sel_r.astype(BF16)
    swap = half * listed
    sel_x_ref[...] = jnp.concatenate([sel_x[:, swap:], sel_x[:, :swap]], axis=1).astype(BF16)
    index = jnp.sum(sel_o * within, axis=1, keepdims=True)
    valid = jnp.sum(sel_o, axis=1, keepdims=True) > 0.5
    fill_hot(hot_ref, index, valid)
    own_ref[...] = jnp.dot(hot_ref[...], table_ref[...], preferred_element_type=F32).astype(BF16)


def ribbon_kernel(near_ref, far_ref, own_ref, sel_r_ref, sel_x_ref, mix_ref, centre_ref, side_ref, out_ref, buffer, sems):
    total, strands, depth = mix_ref.shape
    listed = depth // 2
    slots = total // 2
    core = lax.axis_index("screen")
    rows = jnp.dot(sel_r_ref[...], near_ref[...], preferred_element_type=F32)
    rows = rows + jnp.dot(sel_x_ref[...], far_ref[...], preferred_element_type=F32)
    rows = (rows + own_ref[...].astype(F32)).astype(BF16)
    centre = jnp.dot(rows, centre_ref[0], preferred_element_type=F32).astype(BF16)
    side = jnp.dot(rows, side_ref[0], preferred_element_type=F32).astype(BF16)
    copies = []
    for i in range(total):
        both = jnp.concatenate(
            [centre[i * listed : (i + 1) * listed], side[i * listed : (i + 1) * listed]], axis=0
        )
        buffer[i] = jnp.dot(mix_ref[i], both, preferred_element_type=F32).astype(BF16)
        device = core if i < slots else 1 - core
        place = device * slots + i % slots
        copy = pltpu.make_async_copy(
            buffer.at[i], out_ref.at[pl.ds(pl.multiple_of(place * strands, strands), strands)], sems.at[i]
        )
        copy.start()
        copies.append(copy)
    for copy in copies:
        copy.wait()


def cost(flops, bytes_accessed):
    return pl.CostEstimate(flops=flops, bytes_accessed=bytes_accessed, transcendentals=0)


def shards(guides, neighbours, pick, pick_weight, keep, width, route, tess_centre, tess_side):
    scalps = lax.axis_size("scalp")
    screens = lax.axis_size("screen")
    tile, depth = guides.shape
    blocks, listed = neighbours.shape
    strands = keep.shape[1]
    slots = blocks // screens + blocks // 4
    points = tess_centre.shape[2]
    swap = [(0, 1), (1, 0)]
    both = ("scalp", "screen")
    ask_pairs = []
    for s in range(scalps):
        ask_pairs.append((2 * s, 2 * ((s + 1) % scalps)))
        ask_pairs.append((2 * s + 1, 2 * ((s - 1) % scalps) + 1))
    reply_pairs = [(b, a) for a, b in ask_pairs]

    ask = jnp.concatenate([neighbours, lax.ppermute(neighbours, "screen", swap)], axis=0)
    asked = lax.ppermute(ask, both, ask_pairs)
    all_rows = 2 * blocks * listed
    served = pl.pallas_call(
        serve_kernel,
        out_shape=jax.ShapeDtypeStruct((all_rows, depth), BF16),
        in_specs=[VMEM, VMEM],
        out_specs=VMEM,
        scratch_shapes=[pltpu.VMEM((all_rows, tile), BF16)],
        cost_estimate=cost(2 * all_rows * tile * depth, tile * depth * 2),
        compiler_params=pltpu.CompilerParams(vmem_limit_bytes=LIMIT),
        name="serve",
    )(asked, guides)
    near = lax.ppermute(served, both, reply_pairs)
    packed = pl.pallas_call(
        pack_kernel,
        out_shape=jax.ShapeDtypeStruct((blocks, 16, strands), F32),
        in_specs=[SMEM, VMEM, VMEM, VMEM, VMEM, pl.BlockSpec(memory_space=pl.ANY)],
        out_specs=VMEM,
        cost_estimate=cost(blocks * 16 * strands, blocks * 32 * strands),
        compiler_params=pltpu.CompilerParams(vmem_limit_bytes=LIMIT),
        name="pack",
    )(route[:, 0], pick, pick_weight, keep, width, served)
    theirs = lax.ppermute(packed, "screen", swap)
    total = 2 * slots
    own, sel_r, sel_x, mix = pl.pallas_call(
        functools.partial(plan_kernel, scalps=scalps, slots=slots),
        out_shape=(
            jax.ShapeDtypeStruct((total * listed, depth), BF16),
            jax.ShapeDtypeStruct((total * listed, all_rows), BF16),
            jax.ShapeDtypeStruct((total * listed, all_rows), BF16),
            jax.ShapeDtypeStruct((total, strands, 2 * listed), BF16),
        ),
        in_specs=[VMEM, VMEM, VMEM, VMEM],
        out_specs=(VMEM, VMEM, VMEM, VMEM),
        scratch_shapes=[pltpu.VMEM((total * listed, tile), BF16)],
        cost_estimate=cost(2 * total * listed * tile * depth, tile * depth * 2),
        compiler_params=pltpu.CompilerParams(vmem_limit_bytes=LIMIT),
        name="plan",
    )(ask, packed, theirs, guides)
    near, own = lax.optimization_barrier((near, own))
    far = lax.ppermute(near, "screen", swap)
    return pl.pallas_call(
        ribbon_kernel,
        out_shape=jax.ShapeDtypeStruct((total * strands, points), BF16),
        in_specs=[VMEM] * 8,
        out_specs=pl.BlockSpec(memory_space=pl.ANY),
        scratch_shapes=[pltpu.VMEM((total, strands, points), BF16), pltpu.SemaphoreType.DMA((total,))],
        cost_estimate=cost(2 * total * strands * points * 256, total * strands * points * 2),
        compiler_params=pltpu.CompilerParams(vmem_limit_bytes=LIMIT),
        name="ribbon",
    )(near, far, own, sel_r, sel_x, mix, tess_centre, tess_side)


def solution(mesh):
    return jax.shard_map(
        shards,
        mesh=mesh,
        in_specs=(
            P("scalp", None),
            P(("scalp", "screen"), None),
            P(("scalp", "screen"), None, None),
            P(("scalp", "screen"), None, None),
            P(("scalp", "screen"), None),
            P(("scalp", "screen"), None),
            P(("scalp", "screen"), None),
            P("screen", None, None),
            P("screen", None, None),
        ),
        out_specs=P(("scalp", "screen"), None),
        check_vma=False,
    )
```

time: 126 us -> 43.9 us (0.35)
  waiting for transfers between devices: 59.2 us -> 3.69 us
  other arithmetic: 19.2 us -> 0.69 us
  matrix products: 7.36 us -> 0 us
  blocking collectives: 6.12 us -> 0 us
  Pallas kernels: 0 us -> 5.49 us
  starting transfers between devices: 26 us -> 28.8 us
  local copies, waits for them, and re-layouts: 7.24 us -> 4.64 us
    ppermute x2 -> x5, waiting for transfers between devices: 58.2 us -> 3.69 us  [the longest x1 1.07 us: shards(): far = lax.ppermute(near, 'screen', swap)]
    concatenate x1, other arithmetic: 14.6 us -> 0.69 us  [shards(): jnp.concatenate([neighbours, lax.ppermute(neighbours, 'screen', swap)], a...]
    ppermute x2 -> x5, starting transfers between devices: 18.6 us -> 28.8 us  [the longest x1 10.4 us: shards(): asked = lax.ppermute(ask, both, ask_pairs)]
    all_to_all x2 -> x0, starting transfers between devices: 7.4 us -> none  [the longest x1 4.17 us: shards(): lax.all_to_all(scaled_packed.astype(jnp.bfloat16), 'screen', split_axis=0...]
    dot_general x6 -> x0, matrix products: 7.36 us -> none  [the longest x1 2.82 us: shards(): side = jnp.dot(flat, side_map, preferred_element_type=jnp.float32)]
    all_to_all x1 -> x0, blocking collectives: 6.12 us -> none  [shards(): lax.all_to_all(panel_packed, 'screen', split_axis=0, concat_axis=0, tiled...]
    gather x1 -> x0, local copies, waits for them, and re-layouts: 5.74 us -> none  [shards(): gathered = window[relative * tile + neighbours % tile]]
    pallas_call x0 -> x4, Pallas kernels: none -> 5.49 us  [the longest x1 2.27 us: shards(): pl.pallas_call(ribbon_kernel, out_shape=jax.ShapeDtypeStruct((total * str...]
  transfers between devices with their start and end apart: 4 -> 5, of which waited for: 3 -> 4; matrix products, arithmetic and copies ran while one was open for 6% -> 0% of each run, Pallas kernels for 0% -> 4%
where the time goes in v1:
time: 43.9 us; the launch traced here: 43.4 us
  starting transfers between devices  28.8 us (66%)
  Pallas kernels  5.49 us (13%)
  local copies, waits for them, and re-layouts  4.64 us (11%)
  waiting for transfers between devices  3.69 us (8%)
  other arithmetic  0.69 us (2%)
    ppermute x1, starting transfers between devices, shards(): asked = lax.ppermute(ask, both, ask_pairs)  10.4 us
    ppermute x1, starting transfers between devices, shards(): lax.ppermute(neighbours, 'screen', swap)  8.87 us
    ppermute x1, starting transfers between devices, shards(): theirs = lax.ppermute(packed, 'screen', swap)  5.37 us
    unnamed x18, local copies, waits for them, and re-layouts  4.64 us
    pallas_call x1, Pallas kernels, shards(): pl.pallas_call(ribbon_kernel, out_shape=jax.ShapeDtypeStruct((total * str...  2.27 us
    ppermute x1, starting transfers between devices, shards(): far = lax.ppermute(near, 'screen', swap)  2.26 us
    ppermute x1, starting transfers between devices, shards(): near = lax.ppermute(served, both, reply_pairs)  1.92 us
    pallas_call x1, Pallas kernels, shards(): pl.pallas_call(serve_kernel, out_shape=jax.ShapeDtypeStruct((all_rows, de...  1.32 us
  transfers between devices with their start and end apart: 5, of which 4 were waited for; matrix products, arithmetic and copies ran while one was open for 0% of the time, Pallas kernels for 4%

profile of v1, /device:TPU:1, one launch (start us, length us, event | category | flops | bytes accessed | tf_op | source)
XLA Modules:
  0.0 43.4 jit_solution(13357192288332756541)
XLA Ops:
  0.0 0.0 copy-start.5
  0.0 8.9 %collective-permute-start = (s32[4,32]{1,0:T(4,128)}, s32[4,32]{1,0:T(4,128)S(1)}, u32[]{:S(2)}, u32[]{:S(2)}) collective-permute-start(s32[4,32]{1,0:T(4,128)} %param.10), channel_id=1, source_target_pairs={{0,1},{1,0},{2,3},{3,2},{4,5},{5,4},{6,7},{7,6},{8,9},{9,8},{10,11... | collective-permute-start | bytes 1544 | tf_op jit(solution)/shard_map/ppermute | solution.py:166
  8.9 1.0 %collective-permute-done = s32[4,32]{1,0:T(4,128)S(1)} collective-permute-done((s32[4,32]{1,0:T(4,128)}, s32[4,32]{1,0:T(4,128)S(1)}, u32[]{:S(2)}, u32[]{:S(2)}) %collective-permute-start) | collective-permute-done | bytes 544 | tf_op jit(solution)/shard_map/ppermute | solution.py:166
  9.9 0.7 %pad_add_fusion.ask_ref = s32[8,32]{1,0:T(8,128)S(1)} fusion(s32[4,32]{1,0:T(4,128)S(1)} %collective-permute-done, s32[4,32]{1,0:T(4,128)} %param.10), kind=kLoop, calls=%fused_computation | loop fusion | flops 256 | bytes 2048 | tf_op jit(solution)/shard_map/concatenate | solution.py:166
  10.6 10.4 %collective-permute-start.1 = (s32[8,32]{1,0:T(8,128)S(1)}, s32[8,32]{1,0:T(8,128)S(1)}, u32[]{:S(2)}, u32[]{:S(2)}) collective-permute-start(s32[8,32]{1,0:T(8,128)S(1)} %pad_add_fusion.ask_ref), channel_id=1, source_target_pairs={{0,2},{1,511},{2,4},{3,1},{4,6},{5,3},{6,8},{7,5},{8,10},{9,7},{10... | collective-permute-start | bytes 3080 | tf_op jit(solution)/shard_map/ppermute | solution.py:167
  21.0 0.7 %collective-permute-done.1.ask_ref = s32[8,32]{1,0:T(8,128)S(1)} collective-permute-done((s32[8,32]{1,0:T(8,128)S(1)}, s32[8,32]{1,0:T(8,128)S(1)}, u32[]{:S(2)}, u32[]{:S(2)}) %collective-permute-start.1) | collective-permute-done | bytes 1056 | tf_op jit(solution)/shard_map/ppermute | solution.py:167
  21.7 0.0 copy-start
  21.7 1.9 %copy-done = bf16[4096,384]{1,0:T(8,128)(2,1)S(1)} copy-done((bf16[4096,384]{1,0:T(8,128)(2,1)S(1)}, bf16[4096,384]{1,0:T(8,128)(2,1)}, u32[]{:S(2)}) %copy-start) | copy-done | bytes 3145752
  23.6 0.0 copy-start.1
  23.6 0.0 copy-start.2
  23.6 0.0 copy-start.3
  23.6 1.3 %serve.1.after_ref = bf16[256,384]{1,0:T(8,128)(2,1)S(1)} custom-call(s32[8,32]{1,0:T(8,128)S(1)} %collective-permute-done.1.ask_ref, bf16[4096,384]{1,0:T(8,128)(2,1)S(1)} %copy-done), custom_call_target="tpu_custom_call" | custom-call | flops 805306368 | bytes 3145728 | tf_op jit(solution)/shard_map/serve/pallas_call | solution.py:169
  25.0 1.9 %collective-permute-start.2 = (bf16[256,384]{1,0:T(8,128)(2,1)S(1)}, bf16[256,384]{1,0:T(8,128)(2,1)S(1)}, u32[]{:S(2)}, u32[]{:S(2)}) collective-permute-start(bf16[256,384]{1,0:T(8,128)(2,1)S(1)} %serve.1.after_ref), channel_id=1, source_target_pairs={{2,0},{511,1},{4,2},{1,3},{6,4},{3,5},{8,6},{5,7},{10,8},{7,9},{12... | collective-permute-start | bytes 589832 | tf_op jit(solution)/shard_map/ppermute | solution.py:179
  26.9 0.0 copy-done.5
  26.9 0.0 copy-start.4
  26.9 0.7 %copy-done.4 = s32[4,4,256]{2,1,0:T(4,128)S(1)} copy-done((s32[4,4,256]{2,1,0:T(4,128)S(1)}, s32[4,4,256]{2,1,0:T(4,128)}, u32[]{:S(2)}) %copy-start.4) | copy-done | bytes 16408
  27.6 0.0 copy-start.6
  27.6 0.7 %copy-done.6 = s32[4,256]{1,0:T(4,128)S(1)} copy-done((s32[4,256]{1,0:T(4,128)S(1)}, s32[4,256]{1,0:T(4,128)}, u32[]{:S(2)}) %copy-start.6) | copy-done | bytes 4120
  28.3 0.0 copy-start.7
  28.3 0.7 %copy-done.7 = f32[4,256]{1,0:T(4,128)S(1)} copy-done((f32[4,256]{1,0:T(4,128)S(1)}, f32[4,256]{1,0:T(4,128)}, u32[]{:S(2)}) %copy-start.7) | copy-done | bytes 4120
  29.0 0.0 copy-start.8
  29.0 0.7 %copy-done.8 = s32[4,1]{0,1:T(1,128)S(1)} copy-done((s32[4,1]{0,1:T(1,128)S(1)}, s32[4,1]{0,1:T(1,128)}, u32[]{:S(2)}) %copy-start.8) | copy-done | bytes 40
  29.6 0.6 %pack.1.mine_ref = f32[4,16,256]{2,1,0:T(8,128)S(1)} custom-call(s32[4]{0:T(128)S(1)} %bitcast.1, s32[4,4,256]{2,1,0:T(4,128)S(1)} %copy-done.4, bf16[4,4,256]{2,1,0:T(4,128)(2,1)S(1)} %copy-done.5, s32[4,256]{1,0:T(4,128)S(1)} %copy-done.6, f32[4,256]{1,0:T(4,128)S(1)} %copy-done.7, bf16[256,384]{1,0:T(8,128)(2,1)S(1)} %serve.1.after_ref), custom_call_target="tpu_custom_call" | custom-call | flops 16384 | bytes 32768 | tf_op jit(solution)/shard_map/pack/pallas_call | solution.py:180
  30.3 5.4 %collective-permute-start.3 = (f32[4,16,256]{2,1,0:T(8,128)S(1)}, f32[4,16,256]{2,1,0:T(8,128)S(1)}, u32[]{:S(2)}, u32[]{:S(2)}) collective-permute-start(f32[4,16,256]{2,1,0:T(8,128)S(1)} %pack.1.mine_ref), channel_id=1, source_target_pairs={{0,1},{1,0},{2,3},{3,2},{4,5},{5,4},{6,7},{7,6},{8,9},{9,8},{10,11... | collective-permute-start | bytes 196616 | tf_op jit(solution)/shard_map/ppermute | solution.py:189
  35.7 0.9 %collective-permute-done.3.theirs_ref = f32[4,16,256]{2,1,0:T(8,128)S(1)} collective-permute-done((f32[4,16,256]{2,1,0:T(8,128)S(1)}, f32[4,16,256]{2,1,0:T(8,128)S(1)}, u32[]{:S(2)}, u32[]{:S(2)}) %collective-permute-start.3) | collective-permute-done | bytes 65568 | tf_op jit(solution)/shard_map/ppermute | solution.py:189
  36.5 0.0 copy-done.1
  36.5 1.3 %plan.1 = (bf16[192,384]{1,0:T(8,128)(2,1)S(1)}, bf16[192,256]{1,0:T(8,128)(2,1)S(1)}, bf16[192,256]{1,0:T(8,128)(2,1)S(1)}, bf16[6,256,64]{2,1,0:T(8,128)(2,1)S(1)}) custom-call(s32[8,32]{1,0:T(8,128)S(1)} %pad_add_fusion.ask_ref, f32[4,16,256]{2,1,0:T(8,128)S(1)} %pack.1.mine_ref, f32[4,16,256]{2,1,0:T(8,128)S(1)} %collective-permute-done.3.theirs_ref, ...), custom_call_target="tpu_custom_call" | custom-call | flops 603979776 | bytes 3145728 | tf_op jit(solution)/shard_map/plan/pallas_call | solution.py:191
  37.8 0.0 collective-permute-done.2.near_ref
  37.8 2.3 %collective-permute-start.4 = (bf16[256,384]{1,0:T(8,128)(2,1)S(1)}, bf16[256,384]{1,0:T(8,128)(2,1)S(1)}, u32[]{:S(2)}, u32[]{:S(2)}) collective-permute-start(bf16[256,384]{1,0:T(8,128)(2,1)S(1)} %collective-permute-done.2.near_ref), channel_id=1, source_target_pairs={{0,1},{1,0},{2,3},{3,2},{4,5},{5,4},{6,7},{7,6},{8,9},{9,8},{10,11... | collective-permute-start | bytes 589832 | tf_op jit(solution)/shard_map/ppermute | solution.py:207
  40.1 1.1 %collective-permute-done.4.far_ref = bf16[256,384]{1,0:T(8,128)(2,1)S(1)} collective-permute-done((bf16[256,384]{1,0:T(8,128)(2,1)S(1)}, bf16[256,384]{1,0:T(8,128)(2,1)S(1)}, u32[]{:S(2)}, u32[]{:S(2)}) %collective-permute-start.4) | collective-permute-done | bytes 196640 | tf_op jit(solution)/shard_map/ppermute | solution.py:207
  41.2 0.0 copy-done.2
  41.2 0.0 copy-done.3
  41.2 2.3 %ribbon.1 = bf16[1536,768]{1,0:T(8,128)(2,1)} custom-call(bf16[256,384]{1,0:T(8,128)(2,1)S(1)} %collective-permute-done.2.near_ref, bf16[256,384]{1,0:T(8,128)(2,1)S(1)} %collective-permute-done.4.far_ref, bf16[192,384]{1,0:T(8,128)(2,1)S(1)} %get-tuple-element.13.own_ref, bf16[192,256]{1,0:T(8,128)(2,1)S(1)} %get-tuple-element.14.sel_r_ref, ...), custom_call_target="tpu_custom_call" | custom-call | flops 603979776 | bytes 2359296 | tf_op jit(solution)/shard_map/ribbon/pallas_call | solution.py:208
Async XLA Ops:
  0.0 26.9 %copy-start.5 = (bf16[4,4,256]{2,1,0:T(4,128)(2,1)S(1)}, bf16[4,4,256]{2,1,0:T(4,128)(2,1)}, u32[]{:S(2)}) copy-start(bf16[4,4,256]{2,1,0:T(4,128)(2,1)} %weight_ref.1) | copy-start | bytes 24580
  0.0 9.9 %collective-permute-start = (s32[4,32]{1,0:T(4,128)}, s32[4,32]{1,0:T(4,128)S(1)}, u32[]{:S(2)}, u32[]{:S(2)}) collective-permute-start(s32[4,32]{1,0:T(4,128)} %param.10), channel_id=1, source_target_pairs={{0,1},{1,0},{2,3},{3,2},{4,5},{5,4},{6,7},{7,6},{8,9},{9,8},{10,11... | collective-permute-start | bytes 1544 | tf_op jit(solution)/shard_map/ppermute | solution.py:166
  10.6 11.2 %collective-permute-start.1 = (s32[8,32]{1,0:T(8,128)S(1)}, s32[8,32]{1,0:T(8,128)S(1)}, u32[]{:S(2)}, u32[]{:S(2)}) collective-permute-start(s32[8,32]{1,0:T(8,128)S(1)} %pad_add_fusion.ask_ref), channel_id=1, source_target_pairs={{0,2},{1,511},{2,4},{3,1},{4,6},{5,3},{6,8},{7,5},{8,10},{9,7},{10... | collective-permute-start | bytes 3080 | tf_op jit(solution)/shard_map/ppermute | solution.py:167
  21.7 1.9 %copy-start = (bf16[4096,384]{1,0:T(8,128)(2,1)S(1)}, bf16[4096,384]{1,0:T(8,128)(2,1)}, u32[]{:S(2)}) copy-start(bf16[4096,384]{1,0:T(8,128)(2,1)} %table_ref.3) | copy-start | bytes 9437188
  23.6 12.9 %copy-start.1 = (bf16[4096,384]{1,0:T(8,128)(2,1)S(1)}, bf16[4096,384]{1,0:T(8,128)(2,1)}, u32[]{:S(2)}) copy-start(bf16[4096,384]{1,0:T(8,128)(2,1)} %table_ref.3) | copy-start | bytes 9437188
  23.6 17.5 %copy-start.2 = (bf16[1,384,768]{2,1,0:T(8,128)(2,1)S(1)}, bf16[1,384,768]{2,1,0:T(8,128)(2,1)}, u32[]{:S(2)}) copy-start(bf16[1,384,768]{2,1,0:T(8,128)(2,1)} %centre_ref.1) | copy-start | bytes 1769476
  23.6 17.5 %copy-start.3 = (bf16[1,384,768]{2,1,0:T(8,128)(2,1)S(1)}, bf16[1,384,768]{2,1,0:T(8,128)(2,1)}, u32[]{:S(2)}) copy-start(bf16[1,384,768]{2,1,0:T(8,128)(2,1)} %side_ref.1) | copy-start | bytes 1769476
  25.0 12.9 %collective-permute-start.2 = (bf16[256,384]{1,0:T(8,128)(2,1)S(1)}, bf16[256,384]{1,0:T(8,128)(2,1)S(1)}, u32[]{:S(2)}, u32[]{:S(2)}) collective-permute-start(bf16[256,384]{1,0:T(8,128)(2,1)S(1)} %serve.1.after_ref), channel_id=1, source_target_pairs={{2,0},{511,1},{4,2},{1,3},{6,4},{3,5},{8,6},{5,7},{10,8},{7,9},{12... | collective-permute-start | bytes 589832 | tf_op jit(solution)/shard_map/ppermute | solution.py:179
  26.9 0.7 %copy-start.4 = (s32[4,4,256]{2,1,0:T(4,128)S(1)}, s32[4,4,256]{2,1,0:T(4,128)}, u32[]{:S(2)}) copy-start(s32[4,4,256]{2,1,0:T(4,128)} %pick_ref.1) | copy-start | bytes 49156
  27.6 0.7 %copy-start.6 = (s32[4,256]{1,0:T(4,128)S(1)}, s32[4,256]{1,0:T(4,128)}, u32[]{:S(2)}) copy-start(s32[4,256]{1,0:T(4,128)} %keep_ref.1) | copy-start | bytes 12292
  28.3 0.7 %copy-start.7 = (f32[4,256]{1,0:T(4,128)S(1)}, f32[4,256]{1,0:T(4,128)}, u32[]{:S(2)}) copy-start(f32[4,256]{1,0:T(4,128)} %width_ref.1) | copy-start | bytes 12292
  29.0 0.7 %copy-start.8 = (s32[4,1]{0,1:T(1,128)S(1)}, s32[4,1]{0,1:T(1,128)}, u32[]{:S(2)}) copy-start(s32[4,1]{0,1:T(1,128)} %param.15) | copy-start | bytes 52
  30.3 6.3 %collective-permute-start.3 = (f32[4,16,256]{2,1,0:T(8,128)S(1)}, f32[4,16,256]{2,1,0:T(8,128)S(1)}, u32[]{:S(2)}, u32[]{:S(2)}) collective-permute-start(f32[4,16,256]{2,1,0:T(8,128)S(1)} %pack.1.mine_ref), channel_id=1, source_target_pairs={{0,1},{1,0},{2,3},{3,2},{4,5},{5,4},{6,7},{7,6},{8,9},{9,8},{10,11... | collective-permute-start | bytes 196616 | tf_op jit(solution)/shard_map/ppermute | solution.py:189
  37.8 3.3 %collective-permute-start.4 = (bf16[256,384]{1,0:T(8,128)(2,1)S(1)}, bf16[256,384]{1,0:T(8,128)(2,1)S(1)}, u32[]{:S(2)}, u32[]{:S(2)}) collective-permute-start(bf16[256,384]{1,0:T(8,128)(2,1)S(1)} %collective-permute-done.2.near_ref), channel_id=1, source_target_pairs={{0,1},{1,0},{2,3},{3,2},{4,5},{5,4},{6,7},{7,6},{8,9},{9,8},{10,11... | collective-permute-start | bytes 589832 | tf_op jit(solution)/shard_map/ppermute | solution.py:207
